TPU v7x, 32 devices: a whole 2x2x4 slice. The times are simulated.
32 devices in a mesh: row: 4 (over z), col: 8 (over y, x, core).
Axes of the slice: x: 2, y: 2, z: 4, core: 2. Of those that a mesh axis runs over, the one named last changes fastest.
Arguments:
- block_cells: float32 [352, 5, 16, 256], P(('row', 'col')), may hold values from -0.6 to 1.4, as said below
- slot_blocks: int32 [32, 11], replicated, may hold values from -1 to 191, as said below
Outputs:
- new_cells: float32 [224, 5, 16, 256], P(('row', 'col'))
Inputs may be any that keep to these rules, and one draw needn't show every extreme that they name: `slot_blocks`: row r * 8 + c lists the blocks held by device (r, c): block ids first, in slot order, then -1. Block b belongs to column group b // 24, and every block of column group c is held by exactly one device of that column group. Each device holds 1 to 11 blocks, the devices of a column group hold 24 blocks together, and in every column group one device holds 11 blocks and one holds 1. `block_cells`: fields 0 and 4 (density, pressure) lie in 0.7 to 1.4 and fields 1 to 3 (velocity) in -0.6 to 0.6. Slots marked -1 in slot_blocks hold values that no output depends on.
All inputs are finite; a program needn't handle non-finite values.
Results may differ from a plain program's by a relative error of at most 0.0001.
Values sent between devices are 32-bit elements; how exact they have to be, the bound alone decides.
A program may use at most 64 MiB of HBM per device.

v0:
```python
import functools

import jax
import jax.numpy as jnp
from jax import lax
from jax.experimental import pallas as pl
from jax.experimental.pallas import tpu as pltpu
from jax.sharding import PartitionSpec as P

MESH = pl.DeviceIdType.MESH
BLK_MEAN = 6
OUT = 7
SEND = BLK_MEAN - 1
LANES = 128
DT = 0.12


def make_tables(slot_blocks, rows, cols, my_row, my_col):
    cap = slot_blocks.shape[1]
    levels = rows.bit_length() - 1
    half = rows // 2
    group = BLK_MEAN * rows
    ids = slot_blocks.reshape(rows, cols, cap)
    counts = jnp.sum((ids >= 0).astype(jnp.int32), axis=2)
    row_ids = jnp.arange(rows, dtype=jnp.int32)
    col_ids = jnp.arange(cols, dtype=jnp.int32)
    at_row = jnp.broadcast_to(row_ids[:, None, None], ids.shape)
    at_slot = jnp.broadcast_to(jnp.arange(cap, dtype=jnp.int32), ids.shape)
    mine = (row_ids[:, None] == my_row) & (col_ids[None, :] == my_col)
    scalars = []
    for level in range(levels):
        bit = 1 << level
        other = counts.reshape(rows // (2 * bit), 2, bit, cols)[:, ::-1].reshape(rows, cols)
        send = jnp.maximum(counts - other, 0) // 2
        take = jnp.maximum(other - counts, 0) // 2
        keep = counts - send
        scalars.append(jnp.sum(jnp.where(mine, keep, 0)))
        hit = at_row[None] == row_ids[:, None, None, None]
        keep_here = jnp.sum(jnp.where(hit, keep[:, None, :, None], 0), axis=0)
        other_here = jnp.sum(jnp.where(hit, other[:, None, :, None], 0), axis=0)
        moved = at_slot >= keep_here
        at_row = jnp.where(moved, at_row ^ bit, at_row)
        at_slot = jnp.where(moved, other_here + at_slot - keep_here, at_slot)
        counts = keep + take
    scalars.append(jnp.sum(jnp.where(mine, counts, 0)))
    place = at_row * 16 + at_slot
    origin = row_ids[:, None, None] * 16 + jnp.arange(cap, dtype=jnp.int32)
    origin = jnp.broadcast_to(origin, ids.shape).reshape(-1)
    flat_ids = ids.reshape(-1)
    flat_place = jnp.where(flat_ids >= 0, place.reshape(-1), 0)
    flat_col = jnp.broadcast_to(col_ids[None, :, None], ids.shape).reshape(-1)
    near_far = jnp.stack([my_row, my_row ^ half])
    left, right = (my_col + cols - 1) % cols, (my_col + 1) % cols
    seat_rows = jnp.concatenate([near_far[:1], near_far, near_far])
    seat_cols = jnp.stack([my_col, right, right, left, left])
    seats = (seat_rows[:, None] * 16 + jnp.arange(OUT, dtype=jnp.int32)).reshape(-1, 1)
    seat_cols = jnp.repeat(seat_cols, OUT)[:, None]
    match = (flat_place[None] == seats) & (flat_col[None] == seat_cols) & (flat_ids >= 0)[None]
    along = jnp.sum(jnp.where(match, flat_ids[None] - flat_col[None] * group, 0), axis=1)
    along = along.reshape(5, OUT)
    here, there_right, there_left = along[:1], along[1:3], along[3:5]
    down, up = (lambda a: (a + group - 1) % group), (lambda a: (a + 1) % group)
    mine = jnp.concatenate([left * group + here, left * group + down(here)])
    mine = jnp.concatenate([mine, right * group + here, right * group + up(here)])
    theirs = jnp.concatenate([there_right, down(there_right), there_left, up(there_left)])
    wanted = jnp.concatenate([mine, theirs + my_col * group]).reshape(-1)
    both = flat_place * 4096 + origin
    found = jnp.sum(jnp.where(flat_ids[None] == wanted[:, None], both[None], 0), axis=1)
    source = found ^ (my_row * 16 * 4097)
    source = jnp.concatenate([source & 4095, source >> 12])
    return jnp.concatenate([jnp.stack(scalars), source])


def cell_values(cons):
    rho, mx, my, mz, energy = cons
    inv = 1.0 / rho
    vel = (mx * inv, my * inv, mz * inv)
    p = 0.4 * (energy - 0.5 * rho * (vel[0] * vel[0] + vel[1] * vel[1] + vel[2] * vel[2]))
    theta = p * inv
    sound = jnp.sqrt(1.4 * theta)
    kappa = 0.2 * jnp.exp(0.7 * jnp.log(theta))
    return vel, p, theta, sound, kappa


def conserved(primitive):
    rho, u, v, w, p = primitive
    energy = p / 0.4 + 0.5 * rho * (u * u + v * v + w * w)
    return (rho, rho * u, rho * v, rho * w, energy)


def direction_values(cons, values, normal):
    vel, p, theta, sound, kappa = values
    un = vel[normal]
    flux = [cons[1 + normal], cons[1] * un, cons[2] * un, cons[3] * un, (cons[4] + p) * un]
    flux[1 + normal] = flux[1 + normal] + p
    return (*cons, *flux, jnp.abs(un) + sound, theta, kappa)


def face(low, high):
    half_speed = 0.5 * jnp.maximum(low[10], high[10])
    out = [0.5 * (low[5 + i] + high[5 + i]) - half_speed * (high[i] - low[i]) for i in range(5)]
    out[4] = out[4] - 0.5 * (low[12] + high[12]) * (high[11] - low[11])
    return out


def block_rate(cons, ghost_x, ghost_y):
    edge, flat = cons[0].shape
    row = lax.broadcasted_iota(jnp.int32, (edge, flat), 0)
    lane = lax.broadcasted_iota(jnp.int32, (edge, flat), 1)
    values = cell_values(cons)
    mid = direction_values(cons, values, 0)
    gx = direction_values(ghost_x, cell_values(ghost_x), 0)
    last = row == edge - 1
    up = [
        jnp.where(last, jnp.concatenate([g, g], axis=0), pltpu.roll(m, edge - 1, 0))
        for m, g in zip(mid, gx)
    ]
    upper = face(mid, up)
    bottom = face(gx, [m[:8] for m in mid])
    change = [
        u - jnp.where(row == 0, jnp.concatenate([b, b], axis=0), pltpu.roll(u, 1, 0))
        for u, b in zip(upper, bottom)
    ]
    mid = direction_values(cons, values, 1)
    gy = direction_values(ghost_y, cell_values(ghost_y), 1)
    last = lane >= flat - edge
    up = [
        jnp.where(last, jnp.concatenate([g, g], axis=1), pltpu.roll(m, flat - edge, 1))
        for m, g in zip(mid, gy)
    ]
    upper = face(mid, up)
    bottom = face(gy, [m[:, :LANES] for m in mid])
    change = [
        t + (u - jnp.where(lane < edge, jnp.concatenate([b, b], axis=1), pltpu.roll(u, edge, 1)))
        for t, u, b in zip(change, upper, bottom)
    ]
    mid = direction_values(cons, values, 2)
    up = [pltpu.roll(m, flat - 1, 1) for m in mid]
    upper = face(mid, up)
    height = lane & (edge - 1)
    zero = jnp.zeros_like(values[1])
    wall = [zero, zero, zero, values[1], zero]
    change = [
        t
        + (
            jnp.where(height == edge - 1, w, u)
            - jnp.where(height == 0, w, pltpu.roll(u, 1, 1))
        )
        for t, u, w in zip(change, upper, wall)
    ]
    return [-t for t in change]


def y_units(n):
    return 2 * ((5 * n + 7) // 8)


def units(n):
    return y_units(n) + (10 * n + 7) // 8


def y_seat(slot, f):
    at = slot * 5 + f
    return 2 * (at >> 3), 16 * (at & 7)


def x_seat(n, slot, f, part):
    at = slot * 10 + 2 * f + part
    return y_units(n) + (at >> 3), at & 7


def kernel(rows, cols, cap, *refs):
    levels = rows.bit_length() - 1
    half = rows // 2
    refs = list(refs)
    tab, cells, out = refs[:3]
    refs = refs[3:]
    send_blocks = refs[:levels]
    recv_blocks = refs[levels : 2 * levels]
    refs = refs[2 * levels :]
    start, now = refs[:2]
    sections = [refs[2 + 10 * i : 12 + 10 * i] for i in range(3)]
    bsend, brecv, hsend, hrecv = refs[32:36]
    my_row, my_col = lax.axis_index("row"), lax.axis_index("col")
    left = (my_row, lax.rem(my_col + cols - 1, cols))
    right = (my_row, lax.rem(my_col + 1, cols))

    def partner(level):
        bit = 1 << level
        return (my_row + bit - 2 * bit * (lax.rem(my_row // bit, 2)), my_col)

    barrier = pltpu.get_barrier_semaphore()
    across = partner(levels - 1)[0]
    beside = [(right, left), ((across, right[1]), (across, left[1]))]
    for device in [*beside[0], *beside[1]] + [partner(level) for level in range(levels)]:
        pl.semaphore_signal(barrier, inc=1, device_id=device, device_id_type=MESH)
    pl.semaphore_wait(barrier, 4 + levels)

    def held(slot, depth):
        value = cells[jnp.minimum(slot, cap - 1)]
        for level in range(depth):
            keep = tab[level]
            got = recv_blocks[level][jnp.clip(slot - keep, 0, SEND - 1)]
            value = jnp.where(slot >= keep, got, value)
        return value

    edge, flat = now.shape[2:]
    tile_lane = lax.broadcasted_iota(jnp.int32, (edge, LANES), 1)
    tile_group = tile_lane >> 4
    ghost_row = lax.broadcasted_iota(jnp.int32, (8, 2 * LANES), 0)

    def tile_of(ref, *seat):
        *lead, unit = seat
        return ref[(*lead, pl.ds(unit, 2))].reshape(edge, LANES)

    def put_tile(ref, unit, tile):
        ref[unit : unit + 2] = tile.reshape(2, 8, LANES)

    def move_blocks(level):
        for k in range(SEND):
            send_blocks[level][k] = held(tab[level] + k, level)
        copy = pltpu.make_async_remote_copy(
            src_ref=send_blocks[level],
            dst_ref=recv_blocks[level],
            send_sem=bsend.at[level],
            recv_sem=brecv.at[level],
            device_id=partner(level),
            device_id_type=MESH,
        )
        copy.start()
        return copy

    def remote(step, at, src, dst, device):
        copy = pltpu.make_async_remote_copy(
            src_ref=src,
            dst_ref=dst,
            send_sem=hsend.at[step, at],
            recv_sem=hrecv.at[step, at],
            device_id=device,
            device_id_type=MESH,
        )
        copy.start()
        return copy

    def pack(blocks, n, buffer, high):
        x = edge - 1 if high else 0
        side = slice(LANES, 2 * LANES) if high else slice(0, LANES)
        for first in range(0, 5 * n, 8):
            tile = None
            for at in range(first, min(first + 8, 5 * n)):
                s, f = at // 5, at % 5
                shift = (edge * (at - first) + (edge if high else 0)) % LANES
                piece = blocks[s, f, :, side]
                piece = pltpu.roll(piece, shift, 1) if shift else piece
                tile = piece if tile is None else jnp.where(tile_group == at - first, piece, tile)
            put_tile(buffer, 2 * (first // 8), tile)
        for s in range(n):
            for f in range(5):
                for part in range(2):
                    unit, row = x_seat(n, s, f, part)
                    buffer[unit, row : row + 1, :] = blocks[
                        s, f, x : x + 1, part * LANES : (part + 1) * LANES
                    ]

    base = levels + 1

    def entry(step, kind, far, slot):
        at = kind * OUT if far is None else 4 * OUT + (kind * 2 + far) * OUT
        return tab[base + (12 * OUT if step else 0) + at + slot]

    def near_seat(code):
        return jnp.minimum(code >> 4, half - 1), code & 15

    def select(step, n, known, pick, first_kind, far):
        for s in range(OUT):
            q, sigma = near_seat(entry(step, first_kind, far, s))
            for f in range(5):
                for part in range(2):
                    unit, row = x_seat(n, sigma, f, part)
                    to, at = x_seat(OUT, s, f, part)
                    pick[to, at : at + 1, :] = known[q, unit, pl.ds(row, 1), :]
        seats = [near_seat(entry(step, first_kind + 1, far, s)) for s in range(OUT)]
        for first in range(0, 5 * OUT, 8):
            tile = None
            for at in range(first, min(first + 8, 5 * OUT)):
                q, sigma = seats[at // 5]
                unit, lane = y_seat(sigma, at % 5)
                shift = (edge * (at - first) + LANES - lane) & (LANES - 1)
                piece = pltpu.roll(tile_of(known, q, unit), shift, 1)
                tile = piece if tile is None else jnp.where(tile_group == at - first, piece, tile)
            put_tile(pick, 2 * (first // 8), tile)

    def begin(step, blocks, n):
        flights = []
        for side in range(2):
            known = sections[step][side]
            pack(blocks, n, known.at[0], side == 0)
            if levels > 1:
                flights.append(remote(step, side, known.at[0], known.at[1], partner(0)))
        return flights

    def gather(step, flights):
        for level in range(1, levels - 1):
            size = 1 << level
            for side in range(2):
                known = sections[step][side]
                flights[side].wait()
                flights[side] = remote(
                    step,
                    2 * level + side,
                    known.at[pl.ds(0, size)],
                    known.at[pl.ds(size, size)],
                    partner(level),
                )
        return flights

    def trade(step, n, flights):
        sent = []
        for side in range(2):
            if flights:
                flights[side].wait()
            for far in (1, 0):
                known, pick, sel = (sections[step][at] for at in (side, 2 + 2 * side + far, 6 + 2 * side + far))
                select(step, n, known, pick, 2 * side, far)
                at = 2 * (levels - 1) + 2 * side + far
                sent.append(remote(step, at, pick, sel, beside[far][side]))
        return sent

    def open_block(slot, carry):
        value = held(slot, levels)
        for f, field in enumerate(conserved([value[f] for f in range(5)])):
            start[slot, f] = field
            now[slot, f] = field
        return carry

    def advance(step):
        lo_near, lo_far, hi_near, hi_far = sections[step][6:]

        def run(slot, carry):
            def near(kind):
                return entry(step, kind, None, slot) < 16 * half

            def x_row(close, away, kind, f):
                parts = []
                for part in range(2):
                    unit, row = x_seat(OUT, slot, f, part)
                    a = close[unit, pl.ds(row, 1), :]
                    b = away[unit, pl.ds(row, 1), :]
                    parts.append(jnp.where(near(kind), a, b))
                return jnp.concatenate(parts, axis=1)

            def y_tile(close, away, kind, f, to):
                unit, lane = y_seat(slot, f)
                tile = jnp.where(near(kind), tile_of(close, unit), tile_of(away, unit))
                return pltpu.roll(tile, (LANES + to - lane) & (LANES - 1), 1)

            ghost_x, ghost_y = [], []
            for f in range(5):
                low = x_row(lo_near, lo_far, 0, f)
                high = x_row(hi_near, hi_far, 2, f)
                ghost_x.append(jnp.where(ghost_row == 0, low, high))
                low = y_tile(lo_near, lo_far, 1, f, 0)
                high = y_tile(hi_near, hi_far, 3, f, LANES - edge)
                ghost_y.append(jnp.where(tile_lane < edge, low, high))
            if step == 0:
                ghost_x, ghost_y = conserved(ghost_x), conserved(ghost_y)
            cons = tuple(now[slot, f] for f in range(5))
            rate = block_rate(cons, tuple(ghost_x), tuple(ghost_y))
            moved = [c + DT * d for c, d in zip(cons, rate)]
            if step == 1:
                moved = [0.75 * start[slot, f] + 0.25 * moved[f] for f in range(5)]
            if step == 2:
                moved = [(1.0 / 3.0) * start[slot, f] + (2.0 / 3.0) * moved[f] for f in range(5)]
                rho = moved[0]
                vel = [m / rho for m in moved[1:4]]
                p = 0.4 * (
                    moved[4] - 0.5 * rho * (vel[0] * vel[0] + vel[1] * vel[1] + vel[2] * vel[2])
                )
                filled = slot < tab[levels]
                for f, field in enumerate((rho, *vel, p)):
                    out[slot, f] = jnp.where(filled, field, 0.0)
            else:
                for f in range(5):
                    now[slot, f] = moved[f]
            return carry

        lax.fori_loop(0, OUT, run, 0)

    moving = move_blocks(0)
    flights = begin(0, cells, cap)
    flights = gather(0, flights)
    for level in range(1, levels):
        moving.wait()
        moving = move_blocks(level)
    flights = trade(0, cap, flights)
    moving.wait()
    lax.fori_loop(0, OUT, open_block, 0)
    for step in range(3):
        if step:
            flights = trade(step, OUT, gather(step, begin(step, now, OUT)))
        for flight in flights:
            flight.wait()
        advance(step)


def body(rows, cols, block_cells, slot_blocks):
    cap = slot_blocks.shape[1]
    levels = rows.bit_length() - 1
    half = rows // 2
    edge, flat = block_cells.shape[2:]
    table = make_tables(slot_blocks, rows, cols, lax.axis_index("row"), lax.axis_index("col"))
    block = (5, edge, flat)
    scratch = [pltpu.VMEM((SEND, *block), jnp.float32) for _ in range(2 * levels)]
    scratch += [pltpu.VMEM((OUT, *block), jnp.float32) for _ in range(2)]
    for step in range(3):
        faces = (units(OUT if step else cap), 8, LANES)
        picked = (units(OUT), 8, LANES)
        scratch += [pltpu.VMEM((half, *faces), jnp.float32) for _ in range(2)]
        scratch += [pltpu.VMEM(picked, jnp.float32) for _ in range(8)]
    scratch += [pltpu.SemaphoreType.DMA((levels,)) for _ in range(2)]
    scratch += [pltpu.SemaphoreType.DMA((3, 2 * (levels + 1))) for _ in range(2)]
    return pl.pallas_call(
        functools.partial(kernel, rows, cols, cap),
        out_shape=jax.ShapeDtypeStruct((OUT, *block), jnp.float32),
        in_specs=[
            pl.BlockSpec(memory_space=pltpu.SMEM),
            pl.BlockSpec(memory_space=pltpu.VMEM),
        ],
        out_specs=pl.BlockSpec(memory_space=pltpu.VMEM),
        scratch_shapes=scratch,
        compiler_params=pltpu.CompilerParams(
            collective_id=0, has_side_effects=True, vmem_limit_bytes=32 << 20
        ),
    )(table, block_cells)


def solution(mesh):
    rows, cols = mesh.shape["row"], mesh.shape["col"]
    return jax.shard_map(
        functools.partial(body, rows, cols),
        mesh=mesh,
        in_specs=(P(("row", "col"), None, None, None), P()),
        out_specs=P(("row", "col"), None, None, None),
        check_vma=False,
    )
```

profile of v0, /device:TPU:0, one launch (start us, length us, event | category | flops | bytes accessed | tf_op | source)
XLA Modules:
  0.0 83.3 jit_solution(1089992624742058911)
XLA Ops:
  0.0 0.1 concatenate.23
  0.1 0.1 stack.32
  0.2 0.5 copy-done.1
  0.8 0.1 reduce_sum.105
  0.9 0.1 reshape.495
  1.1 0.1 reduce_sum.103
  1.1 0.8 fusion.2
  2.0 0.1 eq.121
  2.2 0.1 add.276
  2.3 0.1 reduce_sum.111
  2.4 0.1 reshape.499
  2.6 0.1 reduce_sum.109
  2.7 0.1 iota_select_fusion
  2.8 0.1 select_reduce_fusion.1
  2.9 0.1 reduce_sum.115
  3.0 0.1 reduce_sum.113
  3.2 0.1 broadcast_in_dim.130
  3.3 0.1 copy.4
  3.4 0.1 eq.109
  3.5 0.1 eq.119
  3.6 0.1 broadcast_in_dim.132
  3.7 0.1 broadcast_in_dim.122
  3.8 0.2 select_reduce_fusion.5
  4.1 0.1 slice.34
  4.2 0.1 slice.36
  4.3 0.1 concatenate.25
  4.4 0.1 eq.124
  4.5 0.2 select_reduce_fusion
  4.7 2.0 %concatenate.26.refs_0_ = s32[171]{0:T(256)S(1)} concatenate(s32[1]{0:T(128)} %bitcast.1, s32[1]{0:T(128)} %bitcast.4, s32[1]{0:T(128)} %bitcast.5, s32[84]{0:T(128)S(1)} %get-tuple-element.17, s32[84]{0:T(128)S(1)} %get-tuple-element.16), dimensions={0} | concatenate | bytes 1368 | tf_op jit(solution)/shard_map/concatenate | solution.py:71
  6.7 1.2 %copy-done = f32[11,5,16,256]{3,2,1,0:T(8,128)S(1)} copy-done((f32[11,5,16,256]{3,2,1,0:T(8,128)S(1)}, f32[11,5,16,256]{3,2,1,0:T(8,128)}, u32[]{:S(2)}) %copy-start) | copy-done | bytes 901144
  7.9 74.7 %shard_map.28 = f32[7,5,16,256]{3,2,1,0:T(8,128)S(1)} custom-call(s32[171]{0:T(256)S(1)} %concatenate.26.refs_0_, f32[11,5,16,256]{3,2,1,0:T(8,128)S(1)} %copy-done), custom_call_target="tpu_custom_call" | custom-call | tf_op jit(solution)/shard_map/pallas_call | solution.py:422
  82.5 0.8 copy.6
  (27 shorter events, 0.7 us)
Async XLA Ops:
  0.0 0.7 copy-start.1
  6.7 1.2 %copy-start = (f32[11,5,16,256]{3,2,1,0:T(8,128)S(1)}, f32[11,5,16,256]{3,2,1,0:T(8,128)}, u32[]{:S(2)}) copy-start(f32[11,5,16,256]{3,2,1,0:T(8,128)} %refs_1_.1) | copy-start | bytes 2703364
where the time goes:
time: 83.6 us; the launch traced here: 83.3 us
  Pallas kernels  74.7 us (89%)
  local copies, waits for them, and re-layouts  6.79 us (8%)
  other arithmetic  1.74 us (2%)
    pallas_call x1, Pallas kernels, body(): pl.pallas_call(functools.partial(kernel, rows, cols, cap), out_shape=jax....  74.7 us
    unnamed x6, local copies, waits for them, and re-layouts  2.6 us
    concatenate x1, local copies, waits for them, and re-layouts, make_tables(): return jnp.concatenate([jnp.stack(scalars), source])  1.97 us

commit v1 on v0

--- a/solution.py
+++ b/solution.py
@@ -434,10 +434,494 @@
     )(table, block_cells)
 
 
+SIDES = 2
+NEED = 3
+
+
+def swap_lanes(a, lane, step):
+    size = a.shape[1]
+    return jnp.where((lane & step) == 0, pltpu.roll(a, size - step, 1), pltpu.roll(a, step, 1))
+
+
+def seat_tables(slots, scratch, rows, cols, my_row, my_col):
+    cap = slots.shape[1]
+    group = BLK_MEAN * rows
+    span = 16 * rows
+    lane = lax.broadcasted_iota(jnp.int32, (cols, LANES), 1)
+    col = lax.broadcasted_iota(jnp.int32, (cols, LANES), 0)
+    row, slot = (lane >> 4) & (rows - 1), lane & 15
+    ids = jnp.full((cols, LANES), -1, jnp.int32)
+    for r in range(rows):
+        part = slots[r * cols : (r + 1) * cols, :]
+        part = jnp.concatenate([part, jnp.full((cols, LANES - cap), -1, jnp.int32)], axis=1)
+        part = jnp.where(lane < span, part, pltpu.roll(part, span, 1))
+        part = pltpu.roll(part, 16 * r, 1) if r else part
+        ids = jnp.where(row == r, part, ids)
+    held = ids >= 0
+    counts = jnp.where(held, 1, 0)
+    for step in (1, 2, 4, 8):
+        counts = counts + swap_lanes(counts, lane, step)
+    other = swap_lanes(counts, lane, 16)
+    keep = counts - (jnp.maximum(counts - other, 0) >> 1)
+    crossed = slot >= keep
+    at_row = jnp.where(crossed, row ^ 1, row)
+    at_slot = jnp.where(crossed, other + slot - keep, slot)
+    counts = keep + (jnp.maximum(other - counts, 0) >> 1)
+    other = swap_lanes(counts, lane, 32)
+    keep = counts - (jnp.maximum(counts - other, 0) >> 1)
+    keep = jnp.where(crossed, swap_lanes(keep, lane, 16), keep)
+    other = jnp.where(crossed, swap_lanes(other, lane, 16), other)
+    crossed = at_slot >= keep
+    at_row = jnp.where(crossed, at_row ^ 2, at_row)
+    at_slot = jnp.where(crossed, other + at_slot - keep, at_slot)
+    held = held & (lane < span)
+    scratch[0] = jnp.where(held, ids - col * group, -100)
+    scratch[1] = jnp.where(held, at_row * 16 + at_slot, -100)
+
+    def line(kind, c, n):
+        return jnp.broadcast_to(scratch[kind, pl.ds(c, 1), :], (n, LANES))
+
+    def total(mask, value):
+        return jnp.sum(jnp.where(mask, value, 0), axis=1, keepdims=True)
+
+    def down(j):
+        return jnp.where(j <= 0, j + group - 1, j - 1)
+
+    def up(j):
+        return jnp.where(j >= group - 1, j + 1 - group, j + 1)
+
+    left, right = lax.rem(my_col + cols - 1, cols), lax.rem(my_col + 1, cols)
+    n = rows * 8
+    seat = lax.broadcasted_iota(jnp.int32, (n, LANES), 0)
+    lane = lax.broadcasted_iota(jnp.int32, (n, LANES), 1)
+    to_row, target = seat >> 3, (seat >> 3) * 16 + (seat & 7)
+    j_here, f_here = line(0, my_col, n), line(1, my_col, n)
+    code = lane + 64 * f_here
+    on = (f_here >> 4) == to_row
+    columns = [
+        total(f_here == target, lane),
+        total(on & ((lane >> 5) == (to_row >> 1)), 1),
+        total(on & ((lane >> 4) == to_row), 1),
+        total(on, 1),
+    ]
+    for c, moved in ((right, down), (left, up)):
+        j = total(line(1, c, n) == target, line(0, c, n) + 1) - 1
+        columns.append(total(j_here == j, code))
+        columns.append(total(j_here == moved(j), code))
+    first = jnp.zeros((n, LANES), jnp.int32)
+    for at, value in enumerate(columns):
+        first = jnp.where(lane == at, value, first)
+    seat = lax.broadcasted_iota(jnp.int32, (8, LANES), 0)
+    lane = lax.broadcasted_iota(jnp.int32, (8, LANES), 1)
+    j = total(line(1, my_col, 8) == my_row * 16 + seat, line(0, my_col, 8) + 1) - 1
+    second = jnp.zeros((8, LANES), jnp.int32)
+    for at, (c, key) in enumerate(((left, j), (left, down(j)), (right, j), (right, up(j)))):
+        value = total(line(0, c, 8) == key, lane + 64 * line(1, c, 8))
+        second = jnp.where(lane == at, value, second)
+    return jnp.concatenate([first, second], axis=0)
+
+
+def turned(tile, shift, axis):
+    shift %= tile.shape[axis]
+    return pltpu.roll(tile, shift, axis) if shift else tile
+
+
+def pack_face(pieces, at, unit, axis, index):
+    a, b, c, d, e = pieces
+    first = jnp.where(index < 3 * unit, turned(a, -at, axis), turned(b, 3 * unit - at, axis))
+    first = jnp.where(index < 6 * unit, first, turned(c, 6 * unit - at, axis))
+    last = jnp.where(index < 3 * unit, turned(d, -at, axis), turned(e, 3 * unit - at, axis))
+    last = jnp.where(index < 6 * unit, last, turned(c, 4 * unit - at, axis))
+    return first, last
+
+
+def unpack_face(first, last, at, unit, axis, index):
+    third = jnp.where(
+        index < at + 2 * unit,
+        turned(first, at - 6 * unit, axis),
+        turned(last, at - 4 * unit, axis),
+    )
+    return (
+        turned(first, at, axis),
+        turned(first, at - 3 * unit, axis),
+        third,
+        turned(last, at, axis),
+        turned(last, at - 3 * unit, axis),
+    )
+
+
+def section_rate(cons, edge):
+    shape = cons[0].shape
+    height = lax.broadcasted_iota(jnp.int32, shape, 1) & (edge - 1)
+    values = cell_values(cons)
+    change = None
+    for normal, axis, step in ((0, 0, 1), (1, 1, edge), (2, 1, 1)):
+        mid = direction_values(cons, values, normal)
+        up = [pltpu.roll(m, shape[axis] - step, axis) for m in mid]
+        upper = face(mid, up)
+        lower = [pltpu.roll(u, step, axis) for u in upper]
+        if normal == 2:
+            zero = jnp.zeros_like(values[1])
+            wall = [zero, zero, zero, values[1], zero]
+            upper = [jnp.where(height == edge - 1, w, u) for u, w in zip(upper, wall)]
+            lower = [jnp.where(height == 0, w, u) for u, w in zip(lower, wall)]
+        delta = [u - l for u, l in zip(upper, lower)]
+        change = delta if change is None else [t + d for t, d in zip(change, delta)]
+    return [-t for t in change]
+
+
+def wide_kernel(rows, cols, cap, slots, cells_in, out, *refs):
+    refs = list(refs)
+    take = lambda n: [refs.pop(0) for _ in range(n)]
+    (cells, lines, seats, tab) = take(4)
+    packed, chosen, picks = take(4), take(4), [take(4) for _ in range(4)]
+    edge_packed, edge_chosen, edge_picks = take(2), take(2), [take(4) for _ in range(2)]
+    (leaving, beside) = take(2)
+    far_out = [take(2) for _ in range(SEND)]
+    far_in = take(SEND)
+    (halo, start, now) = take(3)
+    (ssem, rsem, lsem) = take(3)
+    edge, flat = out.shape[2:]
+    parts = flat // LANES
+    my_row, my_col = lax.axis_index("row"), lax.axis_index("col")
+    left, right = lax.rem(my_col + cols - 1, cols), lax.rem(my_col + 1, cols)
+    pair = my_row // 2
+    partner = my_row + 1 - 2 * lax.rem(my_row, 2)
+    is_hub = my_row == 1 + pair
+    hub = 1 + pair
+    served = [my_row, partner, rows - 1 - my_row, lax.rem(my_row + 2, rows)]
+    toward = [right, left]
+
+    loading = pltpu.make_async_copy(cells_in, cells, lsem.at[0])
+    loading.start()
+    barrier = pltpu.get_barrier_semaphore()
+    for step in range(1, rows):
+        device = (lax.rem(my_row + step, rows), my_col)
+        pl.semaphore_signal(barrier, inc=1, device_id=device, device_id_type=MESH)
+    for step in range(rows):
+        for c in toward:
+            device = (lax.rem(my_row + step, rows), c)
+            pl.semaphore_signal(barrier, inc=1, device_id=device, device_id_type=MESH)
+    seats[...] = seat_tables(slots, lines, rows, cols, my_row, my_col)
+    seating = pltpu.make_async_copy(seats, tab, lsem.at[1])
+    seating.start()
+
+    def remote(src, dst, send, recv, device):
+        return pltpu.make_async_remote_copy(
+            src_ref=src,
+            dst_ref=dst,
+            send_sem=ssem.at[send],
+            recv_sem=rsem.at[recv],
+            device_id=device,
+            device_id_type=MESH,
+        )
+
+    tile_row = lax.broadcasted_iota(jnp.int32, (8, LANES), 0)
+    tile_lane = lax.broadcasted_iota(jnp.int32, (8, LANES), 1)
+    tall_lane = lax.broadcasted_iota(jnp.int32, (edge, LANES), 1)
+    chunks = [(kind, side) for kind in range(2) for side in range(SIDES)]
+
+    def pack(chunk):
+        kind, side = chunks[chunk]
+        for k in range(cap):
+            for half in range(2):
+                if kind == 0:
+                    at = 0 if side else 8 - NEED
+                    rows_at = pl.ds(0 if side else edge - 8, 8)
+                    pieces = [
+                        cells[k, f, rows_at, half * LANES : (half + 1) * LANES] for f in range(5)
+                    ]
+                    made = pack_face(pieces, at, 1, 0, tile_row)
+                else:
+                    at = 0 if side else LANES - NEED * edge
+                    lanes_at = pl.ds(0 if side else flat - LANES, LANES)
+                    pieces = [cells[k, f, half * 8 : (half + 1) * 8, lanes_at] for f in range(5)]
+                    made = pack_face(pieces, at, edge, 1, tile_lane)
+                for which in range(2):
+                    packed[chunk][1, k, half * 2 + which] = made[which]
+
+    gathers = [
+        remote(packed[c].at[1], packed[c].at[0], c, c, (partner, my_col)) for c in range(4)
+    ]
+    sends = [
+        [
+            remote(
+                picks[c][rel],
+                chosen[c].at[rel // 2],
+                4 + 4 * c + rel,
+                4 + 2 * c + rel // 2,
+                (served[rel], toward[chunks[c][1]]),
+            )
+            for rel in range(4)
+        ]
+        for c in range(4)
+    ]
+    swap = remote(leaving, beside, 20, 12, (partner, my_col))
+    edge_gathers = [
+        remote(edge_packed[i].at[1], edge_packed[i].at[0], 21 + i, 13 + i, (partner, my_col))
+        for i in range(2)
+    ]
+    edge_sends = [
+        [
+            remote(
+                edge_picks[i][rel],
+                edge_chosen[i].at[rel // 2],
+                23 + 4 * i + rel,
+                15 + 2 * i + rel // 2,
+                (served[rel], toward[i]),
+            )
+            for rel in range(4)
+        ]
+        for i in range(2)
+    ]
+    crossings = [
+        [
+            remote(far_out[i][e], far_in[i], 31 + 2 * i + e, 19 + i, (served[2 + e], my_col))
+            for e in range(2)
+        ]
+        for i in range(SEND)
+    ]
+
+    def on_hub(do):
+        pl.when(is_hub)(do)
+
+    def on_edge(do):
+        pl.when(jnp.logical_not(is_hub))(do)
+
+    loading.wait()
+    pack(0)
+    pl.semaphore_wait(barrier, 3 * rows - 1)
+    on_edge(gathers[0].start)
+    for c in range(1, 4):
+        pack(c)
+        on_edge(gathers[c].start)
+
+    seating.wait()
+
+    def entry(row, slot, column):
+        return tab[row * 8 + slot, column]
+
+    def origin(row, slot):
+        code = entry(row, slot, 0)
+        return code >> 4, code & 15
+
+    my_stay = entry(my_row, 0, 2)
+    near_stay = entry(partner, 0, 2)
+    my_base = entry(my_row, 0, 1)
+    for i in range(SEND):
+        leaving[i] = cells[jnp.minimum(my_stay + i, cap - 1)]
+    swap.start()
+
+    def seat_of(place):
+        return jnp.where((place >> 4) == hub, 1, 0), jnp.minimum(place & 15, cap - 1)
+
+    def choose(c):
+        kind, side = chunks[c]
+        gathers[c].wait_recv()
+        for rel in (2, 3, 1, 0):
+            for s in range(OUT):
+                q, k = seat_of(entry(served[rel], s, 4 + 2 * side + kind) & 63)
+                picks[c][rel][s] = packed[c][q, k]
+            sends[c][rel].start()
+
+    @pl.when(is_hub)
+    def _():
+        for c in range(4):
+            choose(c)
+
+    def whose(slot, column, shift):
+        code = (tab[rows * 8 + slot, column] >> shift) & 63
+        return jnp.where((code >> 5) == pair, 0, 1)
+
+    def await_chunk(c):
+        for far in range(2):
+            sends[c][2 * far].wait_recv()
+
+    await_chunk(0)
+    await_chunk(1)
+    corner_group = tile_lane >> 4
+    for s in range(OUT):
+        low, high = whose(s, 0, 0), whose(s, 2, 0)
+        tiles = []
+        for half in range(2):
+            got = []
+            for c, far, at in ((0, low, 8 - NEED), (1, high, 0)):
+                first, last = chosen[c][far, s, half * 2], chosen[c][far, s, half * 2 + 1]
+                got.append(unpack_face(first, last, at, 1, 0, tile_row))
+            tiles.append([jnp.where(tile_row >= 4, a, b) for a, b in zip(*got)])
+            for f in range(5):
+                halo[s, f, half] = tiles[half][f]
+        for side in range(SIDES):
+            source = tiles[0] if side else tiles[parts - 1]
+            made = jnp.zeros((8, LANES), jnp.float32)
+            for f in range(5):
+                one = 0 if side else LANES - edge
+                two = edge if side else LANES - 2 * edge
+                inner = (tile_row == 3) | (tile_row == 4)
+                tile = jnp.where(
+                    inner,
+                    turned(turned(source[f], 4, 0), edge * f - two, 1),
+                    turned(source[f], edge * f - one, 1),
+                )
+                made = jnp.where(corner_group == f, tile, made)
+            edge_packed[side][1, s] = made
+    for side in range(SIDES):
+        on_edge(edge_gathers[side].start)
+
+    def choose_corner(side):
+        edge_gathers[side].wait_recv()
+        for rel in (2, 3, 1, 0):
+            for s in range(OUT):
+                place = (entry(served[rel], s, 5 + 2 * side) >> 6) & 63
+                q, k = seat_of(place)
+                edge_picks[side][rel][s] = edge_packed[side][q, jnp.minimum(k, OUT - 1)]
+            edge_sends[side][rel].start()
+
+    @pl.when(is_hub)
+    def _():
+        for side in range(SIDES):
+            choose_corner(side)
+
+    swap.wait_recv()
+
+    @pl.when(is_hub)
+    def _():
+        for i in range(SEND):
+            for e in range(2):
+                row = served[2 + e]
+                slot = jnp.minimum(entry(row, 0, 1) + i, 7)
+                at_row, k = origin(row, slot)
+                mine = cells[jnp.minimum(k, cap - 1)]
+                near = beside[jnp.clip(k - near_stay, 0, SEND - 1)]
+                far_out[i][e][...] = jnp.where(at_row == my_row, mine, near)
+                crossings[i][e].start()
+
+    await_chunk(2)
+    await_chunk(3)
+    for side in range(SIDES):
+        for far in range(2):
+            edge_sends[side][2 * far].wait_recv()
+
+    filled = entry(my_row, 0, 3)
+
+    def run(s, carry):
+        at_row, k = origin(my_row, s)
+        mine = cells[jnp.minimum(k, cap - 1)]
+        near = beside[jnp.clip(k - near_stay, 0, SEND - 1)]
+        now[:, :edge, :flat] = jnp.where(at_row == my_row, mine, near)
+        for i in range(SEND):
+
+            @pl.when(s == i + 1)
+            def _():
+                crossings[i][0].wait_recv()
+
+            @pl.when(s > i)
+            def _():
+                here = now[:, :edge, :flat]
+                now[:, :edge, :flat] = jnp.where(s - my_base == i, far_in[i][...], here)
+
+        for f in range(5):
+            for half in range(2):
+                now[f, edge:, half * LANES : (half + 1) * LANES] = halo[s, f, half]
+        low, high = whose(s, 1, 0), whose(s, 3, 0)
+        for half in range(2):
+            got = []
+            for c, far, at in ((2, low, LANES - NEED * edge), (3, high, 0)):
+                first, last = chosen[c][far, s, half * 2], chosen[c][far, s, half * 2 + 1]
+                got.append(unpack_face(first, last, at, edge, 1, tile_lane))
+            for f in range(5):
+                now[f, half * 8 : (half + 1) * 8, flat:] = jnp.where(
+                    tile_lane >= LANES // 2, got[0][f], got[1][f]
+                )
+        low = edge_chosen[0][whose(s, 1, 6), s]
+        high = edge_chosen[1][whose(s, 3, 6), s]
+        for f in range(5):
+            a = turned(low, LANES - edge - edge * f, 1)
+            b = turned(turned(low, 4, 0), LANES - 2 * edge - edge * f, 1)
+            c = turned(high, -edge * f, 1)
+            d = turned(turned(high, 4, 0), edge - edge * f, 1)
+            tile = jnp.where(tile_lane < edge, c, d)
+            tile = jnp.where(tile_lane >= LANES // 2, b, tile)
+            now[f, edge:, flat:] = jnp.where(tile_lane >= LANES - edge, a, tile)
+        for f, field in enumerate(conserved([now[f] for f in range(5)])):
+            start[f] = field
+            now[f] = field
+        for step in range(3):
+            cons = tuple(now[f] for f in range(5))
+            rate = section_rate(cons, edge)
+            moved = [c + DT * d for c, d in zip(cons, rate)]
+            if step == 1:
+                moved = [0.75 * start[f] + 0.25 * moved[f] for f in range(5)]
+            if step == 2:
+                moved = [m[:edge, :flat] for m in moved]
+                moved = [
+                    (1.0 / 3.0) * start[f, :edge, :flat] + (2.0 / 3.0) * moved[f] for f in range(5)
+                ]
+                rho = moved[0]
+                vel = [m / rho for m in moved[1:4]]
+                p = 0.4 * (
+                    moved[4] - 0.5 * rho * (vel[0] * vel[0] + vel[1] * vel[1] + vel[2] * vel[2])
+                )
+                for f, field in enumerate((rho, *vel, p)):
+                    out[s, f] = jnp.where(s < filled, field, 0.0)
+            else:
+                for f in range(5):
+                    now[f] = moved[f]
+        return carry
+
+    lax.fori_loop(0, OUT, run, 0)
+    swap.wait_send()
+
+    @pl.when(is_hub)
+    def _():
+        for group in (*sends, *edge_sends, *crossings):
+            for flight in group:
+                flight.wait_send()
+
+    @pl.when(jnp.logical_not(is_hub))
+    def _():
+        for flight in (*gathers, *edge_gathers):
+            flight.wait_send()
+
+
+def wide_body(rows, cols, block_cells, slot_blocks):
+    cap = slot_blocks.shape[1]
+    edge, flat = block_cells.shape[2:]
+    block = (5, edge, flat)
+    f32 = lambda *shape: pltpu.VMEM(shape, jnp.float32)
+    face_tiles = (4, 8, LANES)
+    grown = (5, edge + 8, flat + LANES)
+    scratch = [f32(cap, *block), pltpu.VMEM((2, cols, LANES), jnp.int32)]
+    scratch += [space((rows * 8 + 8, LANES), jnp.int32) for space in (pltpu.VMEM, pltpu.SMEM)]
+    scratch += [f32(2, cap, *face_tiles) for _ in range(4)]
+    scratch += [f32(2, OUT, *face_tiles) for _ in range(4)]
+    scratch += [f32(OUT, *face_tiles) for _ in range(16)]
+    scratch += [f32(2, OUT, 8, LANES) for _ in range(4)]
+    scratch += [f32(OUT, 8, LANES) for _ in range(8)]
+    scratch += [f32(SEND, *block) for _ in range(2)]
+    scratch += [f32(*block) for _ in range(3 * SEND)]
+    scratch += [f32(OUT, 5, 2, 8, LANES), f32(*grown), f32(*grown)]
+    scratch += [pltpu.SemaphoreType.DMA((n,)) for n in (41, 24, 2)]
+    return pl.pallas_call(
+        functools.partial(wide_kernel, rows, cols, cap),
+        out_shape=jax.ShapeDtypeStruct((OUT, *block), jnp.float32),
+        in_specs=[
+            pl.BlockSpec(memory_space=pltpu.VMEM),
+            pl.BlockSpec(memory_space=pl.ANY),
+        ],
+        out_specs=pl.BlockSpec(memory_space=pltpu.VMEM),
+        scratch_shapes=scratch,
+        compiler_params=pltpu.CompilerParams(
+            collective_id=0, has_side_effects=True, vmem_limit_bytes=40 << 20
+        ),
+    )(slot_blocks, block_cells)
+
+
 def solution(mesh):
     rows, cols = mesh.shape["row"], mesh.shape["col"]
+    local = wide_body if (rows, cols) == (4, 8) else body
     return jax.shard_map(
-        functools.partial(body, rows, cols),
+        functools.partial(local, rows, cols),
         mesh=mesh,
         in_specs=(P(("row", "col"), None, None, None), P()),
         out_specs=P(("row", "col"), None, None, None),

time: 83.6 us -> 59.8 us (0.72)
  Pallas kernels: 74.7 us -> 56.8 us
  local copies, waits for them, and re-layouts: 6.79 us -> 2.76 us
  other arithmetic: 1.74 us -> 0 us
    pallas_call x1, Pallas kernels: 74.7 us -> 56.8 us  [wide_body(): pl.pallas_call(functools.partial(wide_kernel, rows, cols, cap), out_shape...]
    concatenate x3 -> x0, local copies, waits for them, and re-layouts: 2.16 us -> none  [the longest x1 1.97 us: make_tables(): return jnp.concatenate([jnp.stack(scalars), source])]
    reduce_sum x7 -> x0, other arithmetic: 1.4 us -> none  [the longest x1 0.79 us: make_tables(): scalars.append(jnp.sum(jnp.where(mine, counts, 0)))]
    unnamed x6 -> x4, local copies, waits for them, and re-layouts: 2.6 us -> 2.76 us
where the time goes in v1:
time: 59.8 us; the launch traced here: 59.6 us
  Pallas kernels  56.8 us (95%)
  local copies, waits for them, and re-layouts  2.76 us (5%)
    pallas_call x1, Pallas kernels, wide_body(): pl.pallas_call(functools.partial(wide_kernel, rows, cols, cap), out_shape...  56.8 us
    unnamed x4, local copies, waits for them, and re-layouts  2.76 us

profile of v1, /device:TPU:0, one launch (start us, length us, event | category | flops | bytes accessed | tf_op | source)
XLA Modules:
  0.0 59.6 jit_solution(10814492907963090805)
XLA Ops:
  0.0 0.8 %copy.3.slots = s32[32,11]{1,0:T(8,128)S(1)} copy(s32[32,11]{0,1:T(8,128)} %param.3) | data formatting | bytes 2816 | tf_op args[1]
  0.8 0.0 copy-start
  0.8 1.2 %copy-done = f32[11,5,16,256]{3,2,1,0:T(8,128)S(1)} copy-done((f32[11,5,16,256]{3,2,1,0:T(8,128)S(1)}, f32[11,5,16,256]{3,2,1,0:T(8,128)}, u32[]{:S(2)}) %copy-start) | copy-done | bytes 901144
  1.9 56.8 %shard_map.28 = f32[7,5,16,256]{3,2,1,0:T(8,128)S(1)} custom-call(s32[32,11]{1,0:T(8,128)S(1)} %copy.3.slots, f32[11,5,16,256]{3,2,1,0:T(8,128)S(1)} %copy-done), custom_call_target="tpu_custom_call" | custom-call | tf_op jit(solution)/shard_map/pallas_call | solution.py:905
  58.8 0.8 %copy.5 = f32[7,5,16,256]{3,2,1,0:T(8,128)} copy(f32[7,5,16,256]{3,2,1,0:T(8,128)S(1)} %shard_map.28) | data formatting | bytes 1146880
Async XLA Ops:
  0.8 1.2 %copy-start = (f32[11,5,16,256]{3,2,1,0:T(8,128)S(1)}, f32[11,5,16,256]{3,2,1,0:T(8,128)}, u32[]{:S(2)}) copy-start(f32[11,5,16,256]{3,2,1,0:T(8,128)} %cells_in.1) | copy-start | bytes 2703364

commit v2 on v1

--- a/solution.py
+++ b/solution.py
@@ -436,6 +436,11 @@
 
 SIDES = 2
 NEED = 3
+PARTS = 8
+LAG = 4
+FORWARD = 2
+LATE = 3
+RELAY = 4
 
 
 def swap_lanes(a, lane, step):
@@ -444,7 +449,10 @@
 
 
 def seat_tables(slots, scratch, rows, cols, my_row, my_col):
-    cap = slots.shape[1]
+    cap, devices = slots.shape
+    slots = jnp.concatenate([slots, jnp.zeros((16 - cap, devices), jnp.int32)], axis=0)
+    slots = jnp.concatenate([slots, jnp.zeros((16, LANES - devices), jnp.int32)], axis=1)
+    slots = jnp.transpose(slots)[:devices, :cap]
     group = BLK_MEAN * rows
     span = 16 * rows
     lane = lax.broadcasted_iota(jnp.int32, (cols, LANES), 1)
@@ -508,6 +516,7 @@
         j = total(line(1, c, n) == target, line(0, c, n) + 1) - 1
         columns.append(total(j_here == j, code))
         columns.append(total(j_here == moved(j), code))
+    columns.append(total(on & ((lane >> 4) == rows - 1 - to_row), 1))
     first = jnp.zeros((n, LANES), jnp.int32)
     for at, value in enumerate(columns):
         first = jnp.where(lane == at, value, first)
@@ -570,15 +579,15 @@
     return [-t for t in change]
 
 
-def wide_kernel(rows, cols, cap, slots, cells_in, out, *refs):
+def wide_kernel(rows, cols, cap, slots, cells, out, *refs):
     refs = list(refs)
     take = lambda n: [refs.pop(0) for _ in range(n)]
-    (cells, lines, seats, tab) = take(4)
-    packed, chosen, picks = take(4), take(4), [take(4) for _ in range(4)]
+    (lines, seats, tab) = take(3)
+    packed, chosen, picks = take(PARTS), take(PARTS), [take(4) for _ in range(PARTS)]
+    merged = take(PARTS)
     edge_packed, edge_chosen, edge_picks = take(2), take(2), [take(4) for _ in range(2)]
-    (leaving, beside) = take(2)
-    far_out = [take(2) for _ in range(SEND)]
-    far_in = take(SEND)
+    (leaving, beside, across) = take(3)
+    far_out, far_in = take(SEND), take(SEND)
     (halo, start, now) = take(3)
     (ssem, rsem, lsem) = take(3)
     edge, flat = out.shape[2:]
@@ -592,8 +601,6 @@
     served = [my_row, partner, rows - 1 - my_row, lax.rem(my_row + 2, rows)]
     toward = [right, left]
 
-    loading = pltpu.make_async_copy(cells_in, cells, lsem.at[0])
-    loading.start()
     barrier = pltpu.get_barrier_semaphore()
     for step in range(1, rows):
         device = (lax.rem(my_row + step, rows), my_col)
@@ -602,8 +609,8 @@
         for c in toward:
             device = (lax.rem(my_row + step, rows), c)
             pl.semaphore_signal(barrier, inc=1, device_id=device, device_id_type=MESH)
-    seats[...] = seat_tables(slots, lines, rows, cols, my_row, my_col)
-    seating = pltpu.make_async_copy(seats, tab, lsem.at[1])
+    seats[...] = seat_tables(slots[...], lines, rows, cols, my_row, my_col)
+    seating = pltpu.make_async_copy(seats, tab, lsem.at[0])
     seating.start()
 
     def remote(src, dst, send, recv, device):
@@ -619,68 +626,63 @@
     tile_row = lax.broadcasted_iota(jnp.int32, (8, LANES), 0)
     tile_lane = lax.broadcasted_iota(jnp.int32, (8, LANES), 1)
     tall_lane = lax.broadcasted_iota(jnp.int32, (edge, LANES), 1)
-    chunks = [(kind, side) for kind in range(2) for side in range(SIDES)]
+    chunks = [(k, side, half) for k in range(2) for half in range(2) for side in range(SIDES)]
 
     def pack(chunk):
-        kind, side = chunks[chunk]
+        kind, side, half = chunks[chunk]
         for k in range(cap):
-            for half in range(2):
-                if kind == 0:
-                    at = 0 if side else 8 - NEED
-                    rows_at = pl.ds(0 if side else edge - 8, 8)
-                    pieces = [
-                        cells[k, f, rows_at, half * LANES : (half + 1) * LANES] for f in range(5)
-                    ]
-                    made = pack_face(pieces, at, 1, 0, tile_row)
-                else:
-                    at = 0 if side else LANES - NEED * edge
-                    lanes_at = pl.ds(0 if side else flat - LANES, LANES)
-                    pieces = [cells[k, f, half * 8 : (half + 1) * 8, lanes_at] for f in range(5)]
-                    made = pack_face(pieces, at, edge, 1, tile_lane)
-                for which in range(2):
-                    packed[chunk][1, k, half * 2 + which] = made[which]
+            if kind == 0:
+                at = 0 if side else 8 - NEED
+                rows_at = pl.ds(0 if side else edge - 8, 8)
+                pieces = [cells[k, f, rows_at, half * LANES : (half + 1) * LANES] for f in range(5)]
+                made = pack_face(pieces, at, 1, 0, tile_row)
+            else:
+                at = 0 if side else LANES - NEED * edge
+                lanes_at = pl.ds(0 if side else flat - LANES, LANES)
+                pieces = [cells[k, f, half * 8 : (half + 1) * 8, lanes_at] for f in range(5)]
+                made = pack_face(pieces, at, edge, 1, tile_lane)
+            for which in range(2):
+                packed[chunk][1, k, which] = made[which]
+
+    used = [0, 0]
+
+    def number(send):
+        used[send] += 1
+        return used[send] - 1
+
+    def to_rows(source, into, column, through=None):
+        recv = [number(0) for _ in range(3)]
+        flights = []
+        for rel in range(4):
+            far, device = rel // 2, (served[rel], column)
+            target = into.at[far]
+            if rel == 3 and through is not None:
+                far, device, target = 2, (served[2], my_col), through
+            flights.append(remote(source[rel], target, number(1), recv[far], device))
+        return flights
 
     gathers = [
-        remote(packed[c].at[1], packed[c].at[0], c, c, (partner, my_col)) for c in range(4)
+        remote(p.at[1], p.at[0], number(1), number(0), (partner, my_col))
+        for p in (*packed, *edge_packed)
     ]
+    gathers, edge_gathers = gathers[:PARTS], gathers[PARTS:]
     sends = [
-        [
-            remote(
-                picks[c][rel],
-                chosen[c].at[rel // 2],
-                4 + 4 * c + rel,
-                4 + 2 * c + rel // 2,
-                (served[rel], toward[chunks[c][1]]),
-            )
-            for rel in range(4)
-        ]
-        for c in range(4)
-    ]
-    swap = remote(leaving, beside, 20, 12, (partner, my_col))
-    edge_gathers = [
-        remote(edge_packed[i].at[1], edge_packed[i].at[0], 21 + i, 13 + i, (partner, my_col))
-        for i in range(2)
+        to_rows(picks[c], chosen[c], toward[chunks[c][1]], merged[c]) for c in range(PARTS)
     ]
     edge_sends = [
-        [
-            remote(
-                edge_picks[i][rel],
-                edge_chosen[i].at[rel // 2],
-                23 + 4 * i + rel,
-                15 + 2 * i + rel // 2,
-                (served[rel], toward[i]),
-            )
-            for rel in range(4)
-        ]
-        for i in range(2)
+        to_rows(edge_picks[i], edge_chosen[i], toward[i]) for i in range(SIDES)
     ]
-    crossings = [
-        [
-            remote(far_out[i][e], far_in[i], 31 + 2 * i + e, 19 + i, (served[2 + e], my_col))
-            for e in range(2)
-        ]
-        for i in range(SEND)
-    ]
+    swap = remote(leaving, beside, number(1), number(0), (partner, my_col))
+    other_hub = (rows - 1 - my_row, my_col)
+    recv = number(0)
+    reach = remote(leaving, across, number(1), recv, other_hub)
+    relay = remote(across, across, number(1), recv, (partner, my_col))
+    crossings, relays = [], []
+    for i in range(SEND):
+        recv = number(0)
+        crossings.append(remote(far_out[i], far_in[i], number(1), recv, other_hub))
+        if i < FORWARD:
+            relays.append(remote(far_in[i], far_in[i], number(1), recv, (partner, my_col)))
 
     def on_hub(do):
         pl.when(is_hub)(do)
@@ -688,14 +690,9 @@
     def on_edge(do):
         pl.when(jnp.logical_not(is_hub))(do)
 
-    loading.wait()
     pack(0)
     pl.semaphore_wait(barrier, 3 * rows - 1)
     on_edge(gathers[0].start)
-    for c in range(1, 4):
-        pack(c)
-        on_edge(gathers[c].start)
-
     seating.wait()
 
     def entry(row, slot, column):
@@ -708,45 +705,81 @@
     my_stay = entry(my_row, 0, 2)
     near_stay = entry(partner, 0, 2)
     my_base = entry(my_row, 0, 1)
-    for i in range(SEND):
-        leaving[i] = cells[jnp.minimum(my_stay + i, cap - 1)]
-    swap.start()
+
+    def fill_leaving():
+        for i in range(SEND):
+            leaving[i] = cells[jnp.minimum(my_stay + i, cap - 1)]
+
+    @pl.when(is_hub)
+    def _():
+        fill_leaving()
+        reach.start()
+        swap.start()
+
+    for c in range(1, PARTS):
+        pack(c)
+        on_edge(gathers[c].start)
+
+    @pl.when(jnp.logical_not(is_hub))
+    def _():
+        fill_leaving()
+        for flight in gathers:
+            flight.wait_send()
+        swap.start()
 
     def seat_of(place):
         return jnp.where((place >> 4) == hub, 1, 0), jnp.minimum(place & 15, cap - 1)
 
     def choose(c):
-        kind, side = chunks[c]
+        kind, side, half = chunks[c]
         gathers[c].wait_recv()
-        for rel in (2, 3, 1, 0):
+        for rel in (3, 2, 0):
             for s in range(OUT):
                 q, k = seat_of(entry(served[rel], s, 4 + 2 * side + kind) & 63)
                 picks[c][rel][s] = packed[c][q, k]
             sends[c][rel].start()
 
+    def merge(c):
+        kind, side, half = chunks[c]
+        sends[c][3].wait_recv()
+        for s in range(OUT):
+            place = entry(partner, s, 4 + 2 * side + kind) & 63
+            q, k = seat_of(place)
+            picks[c][1][s] = jnp.where((place >> 5) == pair, packed[c][q, k], merged[c][s])
+        sends[c][1].start()
+
     @pl.when(is_hub)
     def _():
-        for c in range(4):
-            choose(c)
+        for c in range(PARTS + LAG):
+            if c == RELAY:
+                reach.wait_recv()
+                relay.start()
+            if c < PARTS:
+                choose(c)
+            if c >= LAG:
+                merge(c - LAG)
+
+    hub_flag = jnp.where(is_hub, 1, 0)
 
     def whose(slot, column, shift):
         code = (tab[rows * 8 + slot, column] >> shift) & 63
         return jnp.where((code >> 5) == pair, 0, 1)
 
     def await_chunk(c):
-        for far in range(2):
-            sends[c][2 * far].wait_recv()
-
-    await_chunk(0)
-    await_chunk(1)
+        sends[c][0].wait_recv()
+        on_hub(sends[c][2].wait_recv)
+
+    for c in range(4):
+        await_chunk(c)
     corner_group = tile_lane >> 4
     for s in range(OUT):
-        low, high = whose(s, 0, 0), whose(s, 2, 0)
+        low, high = whose(s, 0, 0) * hub_flag, whose(s, 2, 0) * hub_flag
         tiles = []
         for half in range(2):
             got = []
-            for c, far, at in ((0, low, 8 - NEED), (1, high, 0)):
-                first, last = chosen[c][far, s, half * 2], chosen[c][far, s, half * 2 + 1]
+            for side, far, at in ((0, low, 8 - NEED), (1, high, 0)):
+                c = 2 * half + side
+                first, last = chosen[c][far, s, 0], chosen[c][far, s, 1]
                 got.append(unpack_face(first, last, at, 1, 0, tile_row))
             tiles.append([jnp.where(tile_row >= 4, a, b) for a, b in zip(*got)])
             for f in range(5):
@@ -786,48 +819,71 @@
 
     @pl.when(is_hub)
     def _():
+        hub_row, edge_row = served[2], served[3]
+        onward = entry(edge_row, 0, 8)
+        last = entry(edge_row, 0, 3) - onward
+        hub_base = entry(hub_row, 0, 1)
         for i in range(SEND):
-            for e in range(2):
-                row = served[2 + e]
-                slot = jnp.minimum(entry(row, 0, 1) + i, 7)
-                at_row, k = origin(row, slot)
-                mine = cells[jnp.minimum(k, cap - 1)]
-                near = beside[jnp.clip(k - near_stay, 0, SEND - 1)]
-                far_out[i][e][...] = jnp.where(at_row == my_row, mine, near)
-                crossings[i][e].start()
-
-    await_chunk(2)
-    await_chunk(3)
+            k = jnp.where(
+                i < onward,
+                entry(edge_row, jnp.clip(last + i, 0, 7), 0),
+                entry(hub_row, jnp.clip(hub_base + i - onward, 0, 7), 0),
+            )
+            far_out[i][...] = beside[jnp.clip((k & 15) - near_stay, 0, SEND - 1)]
+            crossings[i].start()
+
+    for c in range(4, PARTS):
+        await_chunk(c)
     for side in range(SIDES):
         for far in range(2):
             edge_sends[side][2 * far].wait_recv()
 
     filled = entry(my_row, 0, 3)
+    onward = entry(pair * (rows - 1), 0, 8)
+    far_stay = entry(rows - 1 - hub, 0, 2)
+    first_far = jnp.where(is_hub, my_base - onward, filled - onward)
+    on_edge(reach.wait_recv)
 
     def run(s, carry):
         at_row, k = origin(my_row, s)
         mine = cells[jnp.minimum(k, cap - 1)]
         near = beside[jnp.clip(k - near_stay, 0, SEND - 1)]
-        now[:, :edge, :flat] = jnp.where(at_row == my_row, mine, near)
+        far = across[jnp.clip(k - far_stay, 0, SEND - 1)]
+        far_hub = at_row == rows - 1 - hub
+        home = jnp.where(at_row == my_row, mine, jnp.where(far_hub, far, near))
+        now[:, :edge, :flat] = home
+        far_edge = at_row == (1 - pair) * (rows - 1)
         for i in range(SEND):
 
-            @pl.when(s == i + 1)
+            @pl.when((s == i + 1) & is_hub)
             def _():
-                crossings[i][0].wait_recv()
-
-            @pl.when(s > i)
+                crossings[i].wait_recv()
+                if i < FORWARD:
+                    relays[i].start()
+
+            if i < FORWARD:
+
+                @pl.when((s == i + LATE) & jnp.logical_not(is_hub))
+                def _():
+                    crossings[i].wait_recv()
+
+            ready = jnp.where(is_hub, i + 1, i + LATE if i < FORWARD else OUT)
+
+            @pl.when(s >= ready)
             def _():
                 here = now[:, :edge, :flat]
-                now[:, :edge, :flat] = jnp.where(s - my_base == i, far_in[i][...], here)
+                chosen_far = far_edge & (s - first_far == i)
+                now[:, :edge, :flat] = jnp.where(chosen_far, far_in[i][...], here)
 
         for f in range(5):
             for half in range(2):
                 now[f, edge:, half * LANES : (half + 1) * LANES] = halo[s, f, half]
-        low, high = whose(s, 1, 0), whose(s, 3, 0)
+        low, high = whose(s, 1, 0) * hub_flag, whose(s, 3, 0) * hub_flag
         for half in range(2):
             got = []
-            for c, far, at in ((2, low, LANES - NEED * edge), (3, high, 0)):
-                first, last = chosen[c][far, s, half * 2], chosen[c][far, s, half * 2 + 1]
+            for side, far, at in ((0, low, LANES - NEED * edge), (1, high, 0)):
+                c = 4 + 2 * half + side
+                first, last = chosen[c][far, s, 0], chosen[c][far, s, 1]
                 got.append(unpack_face(first, last, at, edge, 1, tile_lane))
             for f in range(5):
                 now[f, half * 8 : (half + 1) * 8, flat:] = jnp.where(
@@ -874,13 +930,13 @@
 
     @pl.when(is_hub)
     def _():
-        for group in (*sends, *edge_sends, *crossings):
+        for group in (*sends, *edge_sends, crossings, relays, (reach, relay)):
             for flight in group:
                 flight.wait_send()
 
     @pl.when(jnp.logical_not(is_hub))
     def _():
-        for flight in (*gathers, *edge_gathers):
+        for flight in edge_gathers:
             flight.wait_send()
 
 
@@ -889,32 +945,33 @@
     edge, flat = block_cells.shape[2:]
     block = (5, edge, flat)
     f32 = lambda *shape: pltpu.VMEM(shape, jnp.float32)
-    face_tiles = (4, 8, LANES)
+    face_tiles = (2, 8, LANES)
     grown = (5, edge + 8, flat + LANES)
-    scratch = [f32(cap, *block), pltpu.VMEM((2, cols, LANES), jnp.int32)]
+    scratch = [pltpu.VMEM((2, cols, LANES), jnp.int32)]
     scratch += [space((rows * 8 + 8, LANES), jnp.int32) for space in (pltpu.VMEM, pltpu.SMEM)]
-    scratch += [f32(2, cap, *face_tiles) for _ in range(4)]
-    scratch += [f32(2, OUT, *face_tiles) for _ in range(4)]
-    scratch += [f32(OUT, *face_tiles) for _ in range(16)]
+    scratch += [f32(2, cap, *face_tiles) for _ in range(PARTS)]
+    scratch += [f32(2, OUT, *face_tiles) for _ in range(PARTS)]
+    scratch += [f32(OUT, *face_tiles) for _ in range(4 * PARTS)]
+    scratch += [f32(OUT, *face_tiles) for _ in range(PARTS)]
     scratch += [f32(2, OUT, 8, LANES) for _ in range(4)]
     scratch += [f32(OUT, 8, LANES) for _ in range(8)]
-    scratch += [f32(SEND, *block) for _ in range(2)]
-    scratch += [f32(*block) for _ in range(3 * SEND)]
+    scratch += [f32(SEND, *block) for _ in range(3)]
+    scratch += [f32(*block) for _ in range(2 * SEND)]
     scratch += [f32(OUT, 5, 2, 8, LANES), f32(*grown), f32(*grown)]
-    scratch += [pltpu.SemaphoreType.DMA((n,)) for n in (41, 24, 2)]
+    scratch += [pltpu.SemaphoreType.DMA((n,)) for n in (6 * PARTS + 32, 4 * PARTS + 16, 1)]
     return pl.pallas_call(
         functools.partial(wide_kernel, rows, cols, cap),
         out_shape=jax.ShapeDtypeStruct((OUT, *block), jnp.float32),
         in_specs=[
             pl.BlockSpec(memory_space=pltpu.VMEM),
-            pl.BlockSpec(memory_space=pl.ANY),
+            pl.BlockSpec(memory_space=pltpu.VMEM),
         ],
         out_specs=pl.BlockSpec(memory_space=pltpu.VMEM),
         scratch_shapes=scratch,
         compiler_params=pltpu.CompilerParams(
             collective_id=0, has_side_effects=True, vmem_limit_bytes=40 << 20
         ),
-    )(slot_blocks, block_cells)
+    )(slot_blocks.T, block_cells)
 
 
 def solution(mesh):

time: 59.8 us -> 56.7 us (0.948)
  Pallas kernels: 56.8 us -> 53.9 us
    pallas_call x1, Pallas kernels: 56.8 us -> 53.9 us  [wide_body(): pl.pallas_call(functools.partial(wide_kernel, rows, cols, cap), out_shape...]
    unnamed x4 -> x5, local copies, waits for them, and re-layouts: 2.76 us -> 2.68 us
where the time goes in v2:
time: 56.7 us; the launch traced here: 56.6 us
  Pallas kernels  53.9 us (95%)
  local copies, waits for them, and re-layouts  2.68 us (5%)
    pallas_call x1, Pallas kernels, wide_body(): pl.pallas_call(functools.partial(wide_kernel, rows, cols, cap), out_shape...  53.9 us
    unnamed x5, local copies, waits for them, and re-layouts  2.68 us

profile of v2, /device:TPU:0, one launch (start us, length us, event | category | flops | bytes accessed | tf_op | source)
XLA Modules:
  0.0 56.6 jit_solution(16047540603535463807)
XLA Ops:
  0.0 0.0 copy-start
  0.0 1.2 %copy-done = f32[11,5,16,256]{3,2,1,0:T(8,128)S(1)} copy-done((f32[11,5,16,256]{3,2,1,0:T(8,128)S(1)}, f32[11,5,16,256]{3,2,1,0:T(8,128)}, u32[]{:S(2)}) %copy-start) | copy-done | bytes 901144
  1.2 0.0 copy-start.1
  1.2 0.7 %copy-done.1 = s32[32,11]{0,1:T(8,128)S(1)} copy-done((s32[32,11]{0,1:T(8,128)S(1)}, s32[32,11]{0,1:T(8,128)}, u32[]{:S(2)}) %copy-start.1) | copy-done | bytes 1432
  1.9 53.9 %shard_map.28 = f32[7,5,16,256]{3,2,1,0:T(8,128)S(1)} custom-call(s32[11,32]{1,0:T(8,128)S(1)} %bitcast.1, f32[11,5,16,256]{3,2,1,0:T(8,128)S(1)} %copy-done), custom_call_target="tpu_custom_call" | custom-call | tf_op jit(solution)/shard_map/pallas_call | solution.py:962
  55.7 0.8 %copy.4 = f32[7,5,16,256]{3,2,1,0:T(8,128)} copy(f32[7,5,16,256]{3,2,1,0:T(8,128)S(1)} %shard_map.28) | data formatting | bytes 1146880
Async XLA Ops:
  0.0 1.2 %copy-start = (f32[11,5,16,256]{3,2,1,0:T(8,128)S(1)}, f32[11,5,16,256]{3,2,1,0:T(8,128)}, u32[]{:S(2)}) copy-start(f32[11,5,16,256]{3,2,1,0:T(8,128)} %cells.1) | copy-start | bytes 2703364
  1.2 0.7 %copy-start.1 = (s32[32,11]{0,1:T(8,128)S(1)}, s32[32,11]{0,1:T(8,128)}, u32[]{:S(2)}) copy-start(s32[32,11]{0,1:T(8,128)} %param.3) | copy-start | bytes 4228

commit v3 on v2

--- a/solution.py
+++ b/solution.py
@@ -844,7 +844,8 @@
     first_far = jnp.where(is_hub, my_base - onward, filled - onward)
     on_edge(reach.wait_recv)
 
-    def run(s, carry):
+    def run(turn, carry):
+        s = lax.rem(turn + OUT - 1, OUT)
         at_row, k = origin(my_row, s)
         mine = cells[jnp.minimum(k, cap - 1)]
         near = beside[jnp.clip(k - near_stay, 0, SEND - 1)]
@@ -869,7 +870,7 @@
 
             ready = jnp.where(is_hub, i + 1, i + LATE if i < FORWARD else OUT)
 
-            @pl.when(s >= ready)
+            @pl.when((s >= ready) & (s < OUT - 1))
             def _():
                 here = now[:, :edge, :flat]
                 chosen_far = far_edge & (s - first_far == i)

time: 56.7 us -> 55.6 us (0.981)
  Pallas kernels: 53.9 us -> 52.7 us
    pallas_call x1, Pallas kernels: 53.9 us -> 52.7 us  [wide_body(): pl.pallas_call(functools.partial(wide_kernel, rows, cols, cap), out_shape...]
where the time goes in v3:
time: 55.6 us; the launch traced here: 55.4 us
  Pallas kernels  52.7 us (95%)
  local copies, waits for them, and re-layouts  2.68 us (5%)
    pallas_call x1, Pallas kernels, wide_body(): pl.pallas_call(functools.partial(wide_kernel, rows, cols, cap), out_shape...  52.7 us
    unnamed x5, local copies, waits for them, and re-layouts  2.68 us

profile of v3, /device:TPU:0, one launch (start us, length us, event | category | flops | bytes accessed | tf_op | source)
XLA Modules:
  0.0 55.4 jit_solution(15667646646063179054)
XLA Ops:
  0.0 0.0 copy-start
  0.0 1.2 %copy-done = f32[11,5,16,256]{3,2,1,0:T(8,128)S(1)} copy-done((f32[11,5,16,256]{3,2,1,0:T(8,128)S(1)}, f32[11,5,16,256]{3,2,1,0:T(8,128)}, u32[]{:S(2)}) %copy-start) | copy-done | bytes 901144
  1.2 0.0 copy-start.1
  1.2 0.7 %copy-done.1 = s32[32,11]{0,1:T(8,128)S(1)} copy-done((s32[32,11]{0,1:T(8,128)S(1)}, s32[32,11]{0,1:T(8,128)}, u32[]{:S(2)}) %copy-start.1) | copy-done | bytes 1432
  1.9 52.7 %shard_map.28 = f32[7,5,16,256]{3,2,1,0:T(8,128)S(1)} custom-call(s32[11,32]{1,0:T(8,128)S(1)} %bitcast.1, f32[11,5,16,256]{3,2,1,0:T(8,128)S(1)} %copy-done), custom_call_target="tpu_custom_call" | custom-call | tf_op jit(solution)/shard_map/pallas_call | solution.py:963
  54.6 0.8 %copy.4 = f32[7,5,16,256]{3,2,1,0:T(8,128)} copy(f32[7,5,16,256]{3,2,1,0:T(8,128)S(1)} %shard_map.28) | data formatting | bytes 1146880
Async XLA Ops:
  0.0 1.2 %copy-start = (f32[11,5,16,256]{3,2,1,0:T(8,128)S(1)}, f32[11,5,16,256]{3,2,1,0:T(8,128)}, u32[]{:S(2)}) copy-start(f32[11,5,16,256]{3,2,1,0:T(8,128)} %cells.1) | copy-start | bytes 2703364
  1.2 0.7 %copy-start.1 = (s32[32,11]{0,1:T(8,128)S(1)}, s32[32,11]{0,1:T(8,128)}, u32[]{:S(2)}) copy-start(s32[32,11]{0,1:T(8,128)} %param.3) | copy-start | bytes 4228

commit v4 on v3

--- a/solution.py
+++ b/solution.py
@@ -438,6 +438,8 @@
 NEED = 3
 PARTS = 8
 LAG = 4
+EARLY = 4
+AHEAD = 2
 FORWARD = 2
 LATE = 3
 RELAY = 4
@@ -559,24 +561,52 @@
     )
 
 
-def section_rate(cons, edge):
-    shape = cons[0].shape
-    height = lax.broadcasted_iota(jnp.int32, shape, 1) & (edge - 1)
+def twice_face(low, high):
+    speed = jnp.maximum(low[10], high[10])
+    out = [(low[5 + i] + high[5 + i]) - speed * (high[i] - low[i]) for i in range(5)]
+    out[4] = out[4] - (low[12] + high[12]) * (high[11] - low[11])
+    return out
+
+
+def rolled_side(mid, un, normal, roll):
+    cons, un = [roll(m) for m in mid[:5]], roll(un)
+    speed, theta, kappa = (roll(m) for m in mid[10:])
+    p = theta * cons[0]
+    flux = [cons[1 + normal], cons[1] * un, cons[2] * un, cons[3] * un, (cons[4] + p) * un]
+    flux[1 + normal] = flux[1 + normal] + p
+    return (*cons, *flux, speed, theta, kappa)
+
+
+def cut(values, height, width):
+    if isinstance(values, (tuple, list)):
+        return tuple(cut(v, height, width) for v in values)
+    return values[:height, :width]
+
+
+def twice_change(cons, edge, flat, last):
+    rows, lanes = cons[0].shape
     values = cell_values(cons)
     change = None
     for normal, axis, step in ((0, 0, 1), (1, 1, edge), (2, 1, 1)):
-        mid = direction_values(cons, values, normal)
-        up = [pltpu.roll(m, shape[axis] - step, axis) for m in mid]
-        upper = face(mid, up)
+        tall = edge if last and normal else rows
+        wide = flat if last and normal != 1 else lanes
+        here = cut(values, tall, wide)
+        mid = direction_values(cut(cons, tall, wide), here, normal)
+        size = (tall, wide)[axis]
+        roll = functools.partial(pltpu.roll, shift=size - step, axis=axis)
+        upper = twice_face(mid, rolled_side(mid, here[0][normal], normal, roll))
+        if normal == 2:
+            height = lax.broadcasted_iota(jnp.int32, (tall, wide), 1) & (edge - 1)
+            wall = 2.0 * here[1]
+            walls = [0.0, 0.0, 0.0, wall, 0.0]
+            upper = [jnp.where(height == edge - 1, w, u) for u, w in zip(upper, walls)]
         lower = [pltpu.roll(u, step, axis) for u in upper]
         if normal == 2:
-            zero = jnp.zeros_like(values[1])
-            wall = [zero, zero, zero, values[1], zero]
-            upper = [jnp.where(height == edge - 1, w, u) for u, w in zip(upper, wall)]
-            lower = [jnp.where(height == 0, w, u) for u, w in zip(lower, wall)]
+            lower[3] = jnp.where(height == 0, wall, lower[3])
         delta = [u - l for u, l in zip(upper, lower)]
+        delta = cut(delta, edge, flat) if last else delta
         change = delta if change is None else [t + d for t, d in zip(change, delta)]
-    return [-t for t in change]
+    return change
 
 
 def wide_kernel(rows, cols, cap, slots, cells, out, *refs):
@@ -586,8 +616,8 @@
     packed, chosen, picks = take(PARTS), take(PARTS), [take(4) for _ in range(PARTS)]
     merged = take(PARTS)
     edge_packed, edge_chosen, edge_picks = take(2), take(2), [take(4) for _ in range(2)]
-    (leaving, beside, across) = take(3)
-    far_out, far_in = take(SEND), take(SEND)
+    (leaving, beside) = take(2)
+    across, far_out, far_in = take(SEND), take(SEND), take(SEND)
     (halo, start, now) = take(3)
     (ssem, rsem, lsem) = take(3)
     edge, flat = out.shape[2:]
@@ -674,10 +704,11 @@
     ]
     swap = remote(leaving, beside, number(1), number(0), (partner, my_col))
     other_hub = (rows - 1 - my_row, my_col)
-    recv = number(0)
-    reach = remote(leaving, across, number(1), recv, other_hub)
-    relay = remote(across, across, number(1), recv, (partner, my_col))
-    crossings, relays = [], []
+    reaches, passes, crossings, relays = [], [], [], []
+    for i in range(SEND):
+        recv = number(0)
+        reaches.append(remote(leaving.at[i], across[i], number(1), recv, other_hub))
+        passes.append(remote(across[i], across[i], number(1), recv, (partner, my_col)))
     for i in range(SEND):
         recv = number(0)
         crossings.append(remote(far_out[i], far_in[i], number(1), recv, other_hub))
@@ -713,7 +744,8 @@
     @pl.when(is_hub)
     def _():
         fill_leaving()
-        reach.start()
+        for flight in reaches[:EARLY]:
+            flight.start()
         swap.start()
 
     for c in range(1, PARTS):
@@ -752,8 +784,9 @@
     def _():
         for c in range(PARTS + LAG):
             if c == RELAY:
-                reach.wait_recv()
-                relay.start()
+                for i in range(EARLY):
+                    reaches[i].wait_recv()
+                    passes[i].start()
             if c < PARTS:
                 choose(c)
             if c >= LAG:
@@ -831,6 +864,8 @@
             )
             far_out[i][...] = beside[jnp.clip((k & 15) - near_stay, 0, SEND - 1)]
             crossings[i].start()
+            if EARLY <= i + AHEAD < SEND:
+                reaches[i + AHEAD].start()
 
     for c in range(4, PARTS):
         await_chunk(c)
@@ -842,17 +877,14 @@
     onward = entry(pair * (rows - 1), 0, 8)
     far_stay = entry(rows - 1 - hub, 0, 2)
     first_far = jnp.where(is_hub, my_base - onward, filled - onward)
-    on_edge(reach.wait_recv)
 
     def run(turn, carry):
         s = lax.rem(turn + OUT - 1, OUT)
         at_row, k = origin(my_row, s)
         mine = cells[jnp.minimum(k, cap - 1)]
         near = beside[jnp.clip(k - near_stay, 0, SEND - 1)]
-        far = across[jnp.clip(k - far_stay, 0, SEND - 1)]
         far_hub = at_row == rows - 1 - hub
-        home = jnp.where(at_row == my_row, mine, jnp.where(far_hub, far, near))
-        now[:, :edge, :flat] = home
+        now[:, :edge, :flat] = jnp.where(at_row == my_row, mine, near)
         far_edge = at_row == (1 - pair) * (rows - 1)
         for i in range(SEND):
 
@@ -867,6 +899,23 @@
                 @pl.when((s == i + LATE) & jnp.logical_not(is_hub))
                 def _():
                     crossings[i].wait_recv()
+
+            if i >= EARLY:
+
+                @pl.when((s == i) & is_hub)
+                def _():
+                    reaches[i].wait_recv()
+                    passes[i].start()
+
+            @pl.when((s == i + 1) & jnp.logical_not(is_hub))
+            def _():
+                reaches[i].wait_recv()
+
+            @pl.when((s > i) & (s < OUT - 1))
+            def _():
+                here = now[:, :edge, :flat]
+                chosen_far = far_hub & (k - far_stay == i)
+                now[:, :edge, :flat] = jnp.where(chosen_far, across[i][...], here)
 
             ready = jnp.where(is_hub, i + 1, i + LATE if i < FORWARD else OUT)
 
@@ -905,12 +954,13 @@
             now[f] = field
         for step in range(3):
             cons = tuple(now[f] for f in range(5))
-            rate = section_rate(cons, edge)
-            moved = [c + DT * d for c, d in zip(cons, rate)]
+            change = twice_change(cons, edge, flat, step == 2)
+            if step == 2:
+                cons = cut(cons, edge, flat)
+            moved = [c - (0.5 * DT) * d for c, d in zip(cons, change)]
             if step == 1:
                 moved = [0.75 * start[f] + 0.25 * moved[f] for f in range(5)]
             if step == 2:
-                moved = [m[:edge, :flat] for m in moved]
                 moved = [
                     (1.0 / 3.0) * start[f, :edge, :flat] + (2.0 / 3.0) * moved[f] for f in range(5)
                 ]
@@ -931,7 +981,7 @@
 
     @pl.when(is_hub)
     def _():
-        for group in (*sends, *edge_sends, crossings, relays, (reach, relay)):
+        for group in (*sends, *edge_sends, crossings, relays, reaches, passes):
             for flight in group:
                 flight.wait_send()
 
@@ -956,10 +1006,10 @@
     scratch += [f32(OUT, *face_tiles) for _ in range(PARTS)]
     scratch += [f32(2, OUT, 8, LANES) for _ in range(4)]
     scratch += [f32(OUT, 8, LANES) for _ in range(8)]
-    scratch += [f32(SEND, *block) for _ in range(3)]
-    scratch += [f32(*block) for _ in range(2 * SEND)]
+    scratch += [f32(SEND, *block) for _ in range(2)]
+    scratch += [f32(*block) for _ in range(3 * SEND)]
     scratch += [f32(OUT, 5, 2, 8, LANES), f32(*grown), f32(*grown)]
-    scratch += [pltpu.SemaphoreType.DMA((n,)) for n in (6 * PARTS + 32, 4 * PARTS + 16, 1)]
+    scratch += [pltpu.SemaphoreType.DMA((n,)) for n in (6 * PARTS + 32, 4 * PARTS + 32, 1)]
     return pl.pallas_call(
         functools.partial(wide_kernel, rows, cols, cap),
         out_shape=jax.ShapeDtypeStruct((OUT, *block), jnp.float32),

time: 55.6 us -> 55.4 us (level)
  no operation moved by 1% of the time
where the time goes in v4:
time: 55.4 us; the launch traced here: 55.2 us
  Pallas kernels  52.5 us (95%)
  local copies, waits for them, and re-layouts  2.68 us (5%)
    pallas_call x1, Pallas kernels, wide_body(): pl.pallas_call(functools.partial(wide_kernel, rows, cols, cap), out_shape...  52.5 us
    unnamed x5, local copies, waits for them, and re-layouts  2.68 us

profile of v4, /device:TPU:0, one launch (start us, length us, event | category | flops | bytes accessed | tf_op | source)
XLA Modules:
  0.0 55.2 jit_solution(13566491375055155924)
XLA Ops:
  0.0 0.0 copy-start
  0.0 1.2 %copy-done = f32[11,5,16,256]{3,2,1,0:T(8,128)S(1)} copy-done((f32[11,5,16,256]{3,2,1,0:T(8,128)S(1)}, f32[11,5,16,256]{3,2,1,0:T(8,128)}, u32[]{:S(2)}) %copy-start) | copy-done | bytes 901144
  1.2 0.0 copy-start.1
  1.2 0.7 %copy-done.1 = s32[32,11]{0,1:T(8,128)S(1)} copy-done((s32[32,11]{0,1:T(8,128)S(1)}, s32[32,11]{0,1:T(8,128)}, u32[]{:S(2)}) %copy-start.1) | copy-done | bytes 1432
  1.9 52.5 %shard_map.28 = f32[7,5,16,256]{3,2,1,0:T(8,128)S(1)} custom-call(s32[11,32]{1,0:T(8,128)S(1)} %bitcast.1, f32[11,5,16,256]{3,2,1,0:T(8,128)S(1)} %copy-done), custom_call_target="tpu_custom_call" | custom-call | tf_op jit(solution)/shard_map/pallas_call | solution.py:1013
  54.4 0.8 %copy.4 = f32[7,5,16,256]{3,2,1,0:T(8,128)} copy(f32[7,5,16,256]{3,2,1,0:T(8,128)S(1)} %shard_map.28) | data formatting | bytes 1146880
Async XLA Ops:
  0.0 1.2 %copy-start = (f32[11,5,16,256]{3,2,1,0:T(8,128)S(1)}, f32[11,5,16,256]{3,2,1,0:T(8,128)}, u32[]{:S(2)}) copy-start(f32[11,5,16,256]{3,2,1,0:T(8,128)} %cells.1) | copy-start | bytes 2703364
  1.2 0.7 %copy-start.1 = (s32[32,11]{0,1:T(8,128)S(1)}, s32[32,11]{0,1:T(8,128)}, u32[]{:S(2)}) copy-start(s32[32,11]{0,1:T(8,128)} %param.3) | copy-start | bytes 4228

commit v5 on v4

--- a/solution.py
+++ b/solution.py
@@ -802,6 +802,22 @@
         sends[c][0].wait_recv()
         on_hub(sends[c][2].wait_recv)
 
+    swap.wait_recv()
+
+    @pl.when(is_hub)
+    def _():
+        hub_row, edge_row = served[2], served[3]
+        onward = entry(edge_row, 0, 8)
+        last = entry(edge_row, 0, 3) - onward
+        hub_base = entry(hub_row, 0, 1)
+        for i in range(SEND):
+            k = jnp.where(
+                i < onward,
+                entry(edge_row, jnp.clip(last + i, 0, 7), 0),
+                entry(hub_row, jnp.clip(hub_base + i - onward, 0, 7), 0),
+            )
+            far_out[i][...] = beside[jnp.clip((k & 15) - near_stay, 0, SEND - 1)]
+
     for c in range(4):
         await_chunk(c)
     corner_group = tile_lane >> 4
@@ -848,21 +864,9 @@
         for side in range(SIDES):
             choose_corner(side)
 
-    swap.wait_recv()
-
     @pl.when(is_hub)
     def _():
-        hub_row, edge_row = served[2], served[3]
-        onward = entry(edge_row, 0, 8)
-        last = entry(edge_row, 0, 3) - onward
-        hub_base = entry(hub_row, 0, 1)
         for i in range(SEND):
-            k = jnp.where(
-                i < onward,
-                entry(edge_row, jnp.clip(last + i, 0, 7), 0),
-                entry(hub_row, jnp.clip(hub_base + i - onward, 0, 7), 0),
-            )
-            far_out[i][...] = beside[jnp.clip((k & 15) - near_stay, 0, SEND - 1)]
             crossings[i].start()
             if EARLY <= i + AHEAD < SEND:
                 reaches[i + AHEAD].start()

time: 55.4 us -> 55.4 us (level)
  no operation moved by 1% of the time
where the time goes in v5:
time: 55.4 us; the launch traced here: 55.2 us
  Pallas kernels  52.5 us (95%)
  local copies, waits for them, and re-layouts  2.68 us (5%)
    pallas_call x1, Pallas kernels, wide_body(): pl.pallas_call(functools.partial(wide_kernel, rows, cols, cap), out_shape...  52.5 us
    unnamed x5, local copies, waits for them, and re-layouts  2.68 us

profile of v5, /device:TPU:0, one launch (start us, length us, event | category | flops | bytes accessed | tf_op | source)
XLA Modules:
  0.0 55.2 jit_solution(5941626920943032016)
XLA Ops:
  0.0 0.0 copy-start
  0.0 1.2 %copy-done = f32[11,5,16,256]{3,2,1,0:T(8,128)S(1)} copy-done((f32[11,5,16,256]{3,2,1,0:T(8,128)S(1)}, f32[11,5,16,256]{3,2,1,0:T(8,128)}, u32[]{:S(2)}) %copy-start) | copy-done | bytes 901144
  1.2 0.0 copy-start.1
  1.2 0.7 %copy-done.1 = s32[32,11]{0,1:T(8,128)S(1)} copy-done((s32[32,11]{0,1:T(8,128)S(1)}, s32[32,11]{0,1:T(8,128)}, u32[]{:S(2)}) %copy-start.1) | copy-done | bytes 1432
  1.9 52.5 %shard_map.28 = f32[7,5,16,256]{3,2,1,0:T(8,128)S(1)} custom-call(s32[11,32]{1,0:T(8,128)S(1)} %bitcast.1, f32[11,5,16,256]{3,2,1,0:T(8,128)S(1)} %copy-done), custom_call_target="tpu_custom_call" | custom-call | tf_op jit(solution)/shard_map/pallas_call | solution.py:1017
  54.4 0.8 %copy.4 = f32[7,5,16,256]{3,2,1,0:T(8,128)} copy(f32[7,5,16,256]{3,2,1,0:T(8,128)S(1)} %shard_map.28) | data formatting | bytes 1146880
Async XLA Ops:
  0.0 1.2 %copy-start = (f32[11,5,16,256]{3,2,1,0:T(8,128)S(1)}, f32[11,5,16,256]{3,2,1,0:T(8,128)}, u32[]{:S(2)}) copy-start(f32[11,5,16,256]{3,2,1,0:T(8,128)} %cells.1) | copy-start | bytes 2703364
  1.2 0.7 %copy-start.1 = (s32[32,11]{0,1:T(8,128)S(1)}, s32[32,11]{0,1:T(8,128)}, u32[]{:S(2)}) copy-start(s32[32,11]{0,1:T(8,128)} %param.3) | copy-start | bytes 4228
